TPU v7x, 128 devices: a whole 4x4x4 slice. The times are simulated.
128 devices in a mesh: ctx: 32 (over z_lo, y, x), head: 4 (over z_hi, core).
Axes of the slice: x: 4, y: 4, z: 4 (z_hi: 2, z_lo: 2; z = z_hi * 2 + z_lo), core: 2. Of those that a mesh axis runs over, the one named last changes fastest.
Arguments:
- queries: bfloat16 [1024, 16384], P('ctx', 'head'), may hold values from -512 to 512
- kv_cache: bfloat16 [2, 16384, 1024], P(None, 'ctx', 'head'), may hold values from -7 to 7
- fill_len: int32 [32], P('ctx'), may hold values from 64 to 512
- prompt_offset: int32 [1], replicated, may hold values from 8192 to 15360
Outputs:
- attended: bfloat16 [1024, 16384], P(('ctx', 'head'))
All inputs are finite; a program needn't handle non-finite values.
Results may differ from a plain program's by a relative error of at most 0.0045.
Values may be sent and summed in bfloat16 or wider, within the bound.
No kernel may reach another device: no remote copies, remote signals or barrier semaphores. Data moves between devices by JAX's collectives and lax.ppermute only.
A program may use at most 192 MiB of HBM per device.

v0:
```python
import math
import jax
import jax.numpy as jnp
from jax import lax
from jax.sharding import PartitionSpec as P

HEAD_DIM = 128


def shard_partial(query_rows, key_block, value_block, allowed):
    scaling = 1.0 / math.sqrt(query_rows.shape[-1])
    scores = (
        jnp.einsum("nhgd,khd->hgnk", query_rows, key_block, preferred_element_type=jnp.float32)
        * scaling
    )
    scores = jnp.where(allowed[None, None], scores, -1e30)
    row_max = jnp.max(scores, axis=-1)
    weights = jnp.exp(scores - row_max[..., None])
    row_sum = jnp.sum(weights, axis=-1)
    rounded = weights.astype(jnp.bfloat16)
    weighted = jnp.einsum(
        "hgnk,khd->nhgd", rounded, value_block, preferred_element_type=jnp.float32
    )
    weighted = weighted / jnp.transpose(row_sum, (2, 0, 1))[..., None]
    row_count = query_rows.shape[0]
    partial_value = weighted.astype(jnp.bfloat16).reshape(row_count, -1)
    log_total = jnp.transpose(row_max + jnp.log(row_sum), (2, 0, 1)).reshape(row_count, -1)
    return (partial_value, log_total)


def per_device(queries, kv_cache, fill_len, prompt_offset):
    ctx_size = lax.axis_size("ctx")
    ctx_rank = lax.axis_index("ctx")
    slots = kv_cache.shape[1]
    kv_local = kv_cache.shape[2] // HEAD_DIM
    feat_width = queries.shape[1]
    heads_local = feat_width // HEAD_DIM
    groups = heads_local // kv_local
    slot_ids = jnp.arange(slots, dtype=jnp.int32)
    start_pos = prompt_offset[0]
    key_block = kv_cache[0].reshape(slots, kv_local, HEAD_DIM)
    value_block = kv_cache[1].reshape(slots, kv_local, HEAD_DIM)
    key_pos = ctx_rank * slots + slot_ids
    live_slots = slot_ids < fill_len[0]
    arrived = lax.all_gather(queries, "ctx", axis=0, tiled=True)
    row_count = arrived.shape[0]
    query_pos = start_pos + jnp.arange(row_count, dtype=jnp.int32)
    allowed = live_slots[None, :] & (key_pos[None, :] <= query_pos[:, None])
    partial_value, log_total = shard_partial(
        arrived.reshape(row_count, kv_local, groups, HEAD_DIM), key_block, value_block, allowed
    )
    received = lax.all_to_all(
        partial_value[None], ("ctx", "head"), split_axis=1, concat_axis=0, tiled=True
    )
    received_logs = lax.all_to_all(
        log_total[None], ("ctx", "head"), split_axis=1, concat_axis=0, tiled=True
    )
    head_size = lax.axis_size("head")
    token_rows = received.shape[1]
    received = received.reshape(ctx_size, head_size, token_rows, heads_local, HEAD_DIM)
    received_logs = received_logs.reshape(ctx_size, head_size, token_rows, heads_local)
    log_peak = jnp.max(received_logs, axis=0)
    shares = jnp.exp(received_logs - log_peak[None])
    merged = (
        jnp.sum(shares[..., None] * received.astype(jnp.float32), axis=0)
        / jnp.sum(shares, axis=0)[..., None]
    )
    merged = jnp.transpose(merged, (1, 0, 2, 3)).reshape(token_rows, head_size * feat_width)
    return merged.astype(jnp.bfloat16)


def solution(mesh):
    in_specs = (P("ctx", "head"), P(None, "ctx", "head"), P("ctx"), P())
    out_specs = P(("ctx", "head"), None)
    return jax.shard_map(
        per_device, mesh=mesh, in_specs=in_specs, out_specs=out_specs, check_vma=False
    )
```

profile of v0, /device:TPU:12, one launch (start us, length us, event | category | flops | bytes accessed | tf_op | source)
XLA Modules:
  0.0 589.1 jit_solution(6618123651662183194)
XLA Ops:
  6.5 0.7 all-gather.2.cloned.1.call-update
  8.5 1.1 fusion.13
  9.9 0.4 compare_and_fusion
  10.4 158.9 %all-gather.2.cloned.1.call-done = bf16[1024,4096]{1,0:T(8,128)(2,1)} async-done(((bf16[32,4096]{1,0:T(8,128)(2,1)}), bf16[1024,4096]{1,0:T(8,128)(2,1)}) %all-gather.2.cloned.1.call-update) | async-done | bytes 8388624 | tf_op jit(solution)/shard_map/all_gather | solution.py:45
  169.3 12.0 %copy.32 = bf16[1024,4096]{0,1:T(8,128)(2,1)} copy(bf16[1024,4096]{1,0:T(8,128)(2,1)} %all-gather.2.cloned.1.call-done) | data formatting | bytes 16777216 | tf_op jit(solution)/shard_map/all_gather | solution.py:45
  181.3 28.0 %fusion.2 = (f32[2,16,1024]{2,1,0:T(8,128)S(1)}, f32[2,512,1024,16]{2,1,3,0:T(8,128)}) fusion(pred[1024,512]{0,1:T(8,128)(4,1)S(1)} %compare_and_fusion, bf16[512,2,128,1]{0,2,3,1:T(8,128)(2,1)S(1)} %bitcast.63, bf16[1024,2,16,128]{0,3,2,1:T(8,128)(2,1)} %bitcast.58), kind=kOutput, calls=%fused_computation.4 | convolution fusion | flops 4345266176 | bytes 76414976 | tf_op jit(solution)/shard_map/nhgd,khd->hgnk/dot_general | solution.py:13
  209.3 21.6 %fusion.1 = f32[2,16,1024]{2,1,0:T(8,128)S(1)} fusion(f32[2,512,1024,16]{2,1,3,0:T(8,128)} %get-tuple-element.10, f32[2,16,1024]{2,1,0:T(8,128)S(1)} %get-tuple-element.9, pred[1024,512]{0,1:T(8,128)(4,1)S(1)} %compare_and_fusion), kind=kLoop, calls=%fused_computation.3 | loop fusion | flops 67076096 | bytes 67895296 | tf_op jit(solution)/shard_map/reduce_sum | solution.py:19
  231.3 0.6 broadcast.68
  231.8 1.9 reduce.1
  233.8 0.9 reshape.98
  234.7 16.7 %all-to-all-start = ((f32[128,1,256]{2,1,0:T(1,128)}), f32[128,1,256]{2,1,0:T(1,128)S(1)}, u32[]{:S(2)}, u32[]{:S(2)}) async-start(f32[128,1,256]{2,1,0:T(1,128)} %reshape.98), calls=%async_computation | async-start | bytes 262144 | tf_op jit(solution)/shard_map/all_to_all | solution.py:55
  251.4 28.0 %fusion.6 = bf16[1024,2,16,128]{0,3,2,1:T(8,128)(2,1)} fusion(f32[1024,2,16]{0,2,1:T(8,128)S(1)} %bitcast.65, bf16[512,2,128,1]{0,2,3,1:T(8,128)(2,1)S(1)} %bitcast.67, f32[2,512,1024,16]{2,1,3,0:T(8,128)} %get-tuple-element.10, f32[2,16,1024]{2,1,0:T(8,128)S(1)} %get-tuple-element.9, pred[1024,512]{0,1:T(8,128)(4,1)S(1)} %compare_and_fusion), kind=kOutput, calls=%fused_computation.8 | convolution fusion | flops 4370464768 | bytes 76546048 | tf_op jit(solution)/shard_map/hgnk,khd->nhgd/dot_general | solution.py:21
  279.5 36.5 %copy.38 = bf16[1,1024,4096]{2,0,1:T(2,128)(2,1)} copy(bf16[1,1024,4096]{1,2,0:T(8,128)(2,1)} %bitcast.59) | data formatting | bytes 16777216 | tf_op jit(solution)/shard_map/broadcast_in_dim;reshape | solution.py:53
  316.0 0.5 broadcast.67
  316.5 52.4 %reduce = bf16[1024,4096]{1,0:T(8,128)(2,1)} reduce(bf16[1024,1,4096]{2,1,0:T(2,128)(2,1)} %bitcast.56, bf16[]{:T(256)} %broadcast.67), dimensions={1}, to_apply=%bitcast.45.reduce_sub_computation | reduce | bytes 16777218
  369.0 15.7 %reshape.96 = bf16[128,2,16384]{2,1,0:T(2,128)(2,1)} reshape(bf16[1024,4096]{1,0:T(8,128)(2,1)} %reduce) | data formatting | bytes 16777216
  384.7 10.2 %all-to-all-start.1 = ((bf16[128,2,16384]{2,1,0:T(2,128)(2,1)}), bf16[128,2,16384]{2,1,0:T(2,128)(2,1)}, u32[]{:S(2)}, u32[]{:S(2)}) async-start(bf16[128,2,16384]{2,1,0:T(2,128)(2,1)} %reshape.96), calls=%async_computation.1 | async-start | bytes 16777216 | tf_op jit(solution)/shard_map/all_to_all | solution.py:52
  394.9 0.9 reduce.2
  395.8 0.9 reshape.99
  396.9 121.9 %all-to-all-done.1 = bf16[128,2,16384]{2,1,0:T(2,128)(2,1)} async-done(((bf16[128,2,16384]{2,1,0:T(2,128)(2,1)}), bf16[128,2,16384]{2,1,0:T(2,128)(2,1)}, u32[]{:S(2)}, u32[]{:S(2)}) %all-to-all-start.1) | async-done | bytes 8388640 | tf_op jit(solution)/shard_map/all_to_all | solution.py:52
  518.8 38.4 %reshape.97 = bf16[1024,1,4096]{2,1,0:T(2,128)(2,1)} reshape(bf16[128,2,16384]{2,1,0:T(2,128)(2,1)} %all-to-all-done.1) | data formatting | bytes 16777216
  557.2 18.9 %bitcast_convert_fusion = f32[1,1024,4096]{2,0,1:T(1,128)S(1)} fusion(bf16[1024,1,4096]{2,1,0:T(2,128)(2,1)} %reshape.97), kind=kLoop, calls=%fused_computation.23 | loop fusion | flops 4194304 | bytes 25165824 | tf_op jit(solution)/shard_map/convert_element_type | solution.py:65
  576.1 5.1 multiply_reduce_fusion
  581.4 0.9 copy.49
  (13 shorter events, 1.0 us)
Async XLA Ops:
  6.5 162.8 %all-gather.2.cloned.1.call-start = ((), (), s32[]{:S(2)}) async-start(), calls=%async_computation.2 | async-start | bytes 8650752 | tf_op jit(solution)/shard_map/all_gather | solution.py:45
  234.7 150.0 %all-to-all-start = ((f32[128,1,256]{2,1,0:T(1,128)}), f32[128,1,256]{2,1,0:T(1,128)S(1)}, u32[]{:S(2)}, u32[]{:S(2)}) async-start(f32[128,1,256]{2,1,0:T(1,128)} %reshape.98), calls=%async_computation | async-start | bytes 262144 | tf_op jit(solution)/shard_map/all_to_all | solution.py:55
  384.7 134.1 %all-to-all-start.1 = ((bf16[128,2,16384]{2,1,0:T(2,128)(2,1)}), bf16[128,2,16384]{2,1,0:T(2,128)(2,1)}, u32[]{:S(2)}, u32[]{:S(2)}) async-start(bf16[128,2,16384]{2,1,0:T(2,128)(2,1)} %reshape.96), calls=%async_computation.1 | async-start | bytes 16777216 | tf_op jit(solution)/shard_map/all_to_all | solution.py:52
Sparse Core Ops, SparseCore 0:
  9.0 160.2 all-gather.1
where the time goes:
time: 592 us; the launch traced here: 589 us
  waiting for transfers between devices  282 us (48%)
  local copies, waits for them, and re-layouts  108 us (18%)
  other arithmetic  102 us (17%)
  matrix products  56 us (9%)
  starting transfers between devices  27 us (5%)
  between operations  14.8 us (2%)
    all_gather x1, waiting for transfers between devices, per_device(): arrived = lax.all_gather(queries, 'ctx', axis=0, tiled=True)  159 us
    all_to_all x1, waiting for transfers between devices, per_device(): lax.all_to_all(partial_value[None], ('ctx', 'head'), split_axis=1, concat...  122 us
    unnamed x8, local copies, waits for them, and re-layouts  58 us
    unnamed x2, other arithmetic  54.4 us
    another operation x1, local copies, waits for them, and re-layouts, per_device(): partial_value[None]  36.5 us
    dot_general x1, matrix products, shard_partial(): jnp.einsum('hgnk,khd->nhgd', rounded, value_block, preferred_element_type...  28 us
    dot_general x1, matrix products, shard_partial(): jnp.einsum('nhgd,khd->hgnk', query_rows, key_block, preferred_element_typ...  28 us
    reduce_sum x1, other arithmetic, shard_partial(): row_sum = jnp.sum(weights, axis=-1)  21.6 us
  transfers between devices with their start and end apart: 3, of which 2 were waited for; matrix products, arithmetic and copies ran while one was open for 23% of the time, Pallas kernels for 0%

commit v1 on v0

--- a/solution.py
+++ b/solution.py
@@ -42,7 +42,9 @@
     value_block = kv_cache[1].reshape(slots, kv_local, HEAD_DIM)
     key_pos = ctx_rank * slots + slot_ids
     live_slots = slot_ids < fill_len[0]
-    arrived = lax.all_gather(queries, "ctx", axis=0, tiled=True)
+    arrived = jnp.concatenate(
+        lax.all_to_all(jnp.stack([queries] * lax.axis_size("ctx")), "ctx", 0, 0), axis=0
+    )
     row_count = arrived.shape[0]
     query_pos = start_pos + jnp.arange(row_count, dtype=jnp.int32)
     allowed = live_slots[None, :] & (key_pos[None, :] <= query_pos[:, None])

time: 592 us -> 552 us (0.932)
  waiting for transfers between devices: 282 us -> 242 us
  between operations: 14.8 us -> 1.47 us
    all_gather x1 -> x0, waiting for transfers between devices: 159 us -> none  [per_device(): arrived = lax.all_gather(queries, 'ctx', axis=0, tiled=True)]
    all_to_all x0 -> x1, waiting for transfers between devices: none -> 120 us  [per_device(): lax.all_to_all(jnp.stack([queries] * lax.axis_size('ctx')), 'ctx', 0, 0)]
    all_gather x1 -> x0, local copies, waits for them, and re-layouts: 12 us -> none  [per_device(): arrived = lax.all_gather(queries, 'ctx', axis=0, tiled=True)]
    unnamed x8 -> x11, local copies, waits for them, and re-layouts: 58 us -> 67.4 us
    all_to_all x0 -> x1, starting transfers between devices: none -> 8.89 us  [per_device(): lax.all_to_all(jnp.stack([queries] * lax.axis_size('ctx')), 'ctx', 0, 0)]
  transfers between devices with their start and end apart: 3 -> 3, of which waited for: 2 -> 2; matrix products, arithmetic and copies ran while one was open for 23% -> 25% of each run, Pallas kernels for 0% -> 0%
where the time goes in v1:
time: 552 us; the launch traced here: 549 us
  waiting for transfers between devices  242 us (44%)
  local copies, waits for them, and re-layouts  110 us (20%)
  other arithmetic  102 us (18%)
  matrix products  61.7 us (11%)
  starting transfers between devices  32.6 us (6%)
    all_to_all x1, waiting for transfers between devices, per_device(): lax.all_to_all(partial_value[None], ('ctx', 'head'), split_axis=1, concat...  122 us
    all_to_all x1, waiting for transfers between devices, per_device(): lax.all_to_all(jnp.stack([queries] * lax.axis_size('ctx')), 'ctx', 0, 0)  120 us
    unnamed x11, local copies, waits for them, and re-layouts  67.4 us
    unnamed x2, other arithmetic  54.4 us
    another operation x1, local copies, waits for them, and re-layouts, per_device(): partial_value[None]  36.5 us
    dot_general x1, matrix products, shard_partial(): jnp.einsum('nhgd,khd->hgnk', query_rows, key_block, preferred_element_typ...  33.7 us
    dot_general x1, matrix products, shard_partial(): jnp.einsum('hgnk,khd->nhgd', rounded, value_block, preferred_element_type...  28 us
    reduce_sum x1, other arithmetic, shard_partial(): row_sum = jnp.sum(weights, axis=-1)  21.6 us
  transfers between devices with their start and end apart: 3, of which 2 were waited for; matrix products, arithmetic and copies ran while one was open for 25% of the time, Pallas kernels for 0%

profile of v1, /device:TPU:12, one launch (start us, length us, event | category | flops | bytes accessed | tf_op | source)
XLA Modules:
  0.0 548.9 jit_solution(7672688280537967251)
XLA Ops:
  0.0 5.3 stack.2
  5.3 8.9 %all-to-all-start = ((bf16[32,32,4096]{2,1,0:T(8,128)(2,1)}), bf16[32,32,4096]{2,1,0:T(8,128)(2,1)}, u32[]{:S(2)}, u32[]{:S(2)}) async-start(bf16[32,32,4096]{2,1,0:T(8,128)(2,1)} %stack.2), calls=%async_computation | async-start | bytes 16777216 | tf_op jit(solution)/shard_map/all_to_all | solution.py:46
  15.8 0.4 compare_and_fusion
  16.3 119.9 %all-to-all-done = bf16[32,32,4096]{2,1,0:T(8,128)(2,1)} async-done(((bf16[32,32,4096]{2,1,0:T(8,128)(2,1)}), bf16[32,32,4096]{2,1,0:T(8,128)(2,1)}, u32[]{:S(2)}, u32[]{:S(2)}) %all-to-all-start) | async-done | bytes 8388640 | tf_op jit(solution)/shard_map/all_to_all | solution.py:46
  136.1 9.4 %copy.42 = bf16[128,8,32,128]{3,2,1,0:T(8,128)(2,1)} copy(bf16[128,8,32,128]{3,1,2,0:T(8,128)(2,1)} %bitcast.23) | data formatting | bytes 16777216
  145.5 33.7 %fusion.2 = (f32[2,16,1024]{2,1,0:T(8,128)S(1)}, f32[2,512,1024,16]{2,1,3,0:T(8,128)}) fusion(pred[1024,512]{0,1:T(8,128)(4,1)S(1)} %compare_and_fusion, bf16[512,2,128,1]{0,2,3,1:T(8,128)(2,1)S(1)} %bitcast.65, bf16[1024,2,16,128]{3,2,1,0:T(8,128)(2,1)} %bitcast.60), kind=kOutput, calls=%fused_computation.4 | convolution fusion | flops 4345266176 | bytes 76414976 | tf_op jit(solution)/shard_map/nhgd,khd->hgnk/dot_general | solution.py:13
  179.2 21.6 %fusion.1 = f32[2,16,1024]{2,1,0:T(8,128)S(1)} fusion(f32[2,512,1024,16]{2,1,3,0:T(8,128)} %get-tuple-element.10, f32[2,16,1024]{2,1,0:T(8,128)S(1)} %get-tuple-element.9, pred[1024,512]{0,1:T(8,128)(4,1)S(1)} %compare_and_fusion), kind=kLoop, calls=%fused_computation.3 | loop fusion | flops 67076096 | bytes 67895296 | tf_op jit(solution)/shard_map/reduce_sum | solution.py:19
  201.2 0.6 broadcast.70
  201.8 1.9 reduce.1
  203.7 0.9 reshape.96
  204.6 13.5 %all-to-all-start.1 = ((f32[128,1,256]{2,1,0:T(1,128)}), f32[128,1,256]{2,1,0:T(1,128)S(1)}, u32[]{:S(2)}, u32[]{:S(2)}) async-start(f32[128,1,256]{2,1,0:T(1,128)} %reshape.96), calls=%async_computation.1 | async-start | bytes 262144 | tf_op jit(solution)/shard_map/all_to_all | solution.py:57
  218.1 28.0 %fusion.6 = bf16[1024,2,16,128]{0,3,2,1:T(8,128)(2,1)} fusion(f32[1024,2,16]{0,2,1:T(8,128)S(1)} %bitcast.67, bf16[512,2,128,1]{0,2,3,1:T(8,128)(2,1)S(1)} %bitcast.69, f32[2,512,1024,16]{2,1,3,0:T(8,128)} %get-tuple-element.10, f32[2,16,1024]{2,1,0:T(8,128)S(1)} %get-tuple-element.9, pred[1024,512]{0,1:T(8,128)(4,1)S(1)} %compare_and_fusion), kind=kOutput, calls=%fused_computation.8 | convolution fusion | flops 4370464768 | bytes 76546048 | tf_op jit(solution)/shard_map/hgnk,khd->nhgd/dot_general | solution.py:21
  246.1 36.5 %copy.34 = bf16[1,1024,4096]{2,0,1:T(2,128)(2,1)} copy(bf16[1,1024,4096]{1,2,0:T(8,128)(2,1)} %bitcast.61) | data formatting | bytes 16777216 | tf_op jit(solution)/shard_map/broadcast_in_dim;reshape | solution.py:55
  282.7 0.5 broadcast.69
  283.2 52.4 %reduce = bf16[1024,4096]{1,0:T(8,128)(2,1)} reduce(bf16[1024,1,4096]{2,1,0:T(2,128)(2,1)} %bitcast.58, bf16[]{:T(256)} %broadcast.69), dimensions={1}, to_apply=%bitcast.48.reduce_sub_computation | reduce | bytes 16777218
  335.6 15.7 %reshape.94 = bf16[128,2,16384]{2,1,0:T(2,128)(2,1)} reshape(bf16[1024,4096]{1,0:T(8,128)(2,1)} %reduce) | data formatting | bytes 16777216
  351.3 10.2 %all-to-all-start.2 = ((bf16[128,2,16384]{2,1,0:T(2,128)(2,1)}), bf16[128,2,16384]{2,1,0:T(2,128)(2,1)}, u32[]{:S(2)}, u32[]{:S(2)}) async-start(bf16[128,2,16384]{2,1,0:T(2,128)(2,1)} %reshape.94), calls=%async_computation.2 | async-start | bytes 16777216 | tf_op jit(solution)/shard_map/all_to_all | solution.py:54
  361.6 0.9 reduce.2
  362.5 0.9 reshape.97
  363.6 121.9 %all-to-all-done.2 = bf16[128,2,16384]{2,1,0:T(2,128)(2,1)} async-done(((bf16[128,2,16384]{2,1,0:T(2,128)(2,1)}), bf16[128,2,16384]{2,1,0:T(2,128)(2,1)}, u32[]{:S(2)}, u32[]{:S(2)}) %all-to-all-start.2) | async-done | bytes 8388640 | tf_op jit(solution)/shard_map/all_to_all | solution.py:54
  485.4 38.4 %reshape.95 = bf16[1024,1,4096]{2,1,0:T(2,128)(2,1)} reshape(bf16[128,2,16384]{2,1,0:T(2,128)(2,1)} %all-to-all-done.2) | data formatting | bytes 16777216
  523.8 18.9 %bitcast_convert_fusion = f32[1,1024,4096]{2,0,1:T(1,128)S(1)} fusion(bf16[1024,1,4096]{2,1,0:T(2,128)(2,1)} %reshape.95), kind=kLoop, calls=%fused_computation.25 | loop fusion | flops 4194304 | bytes 25165824 | tf_op jit(solution)/shard_map/convert_element_type | solution.py:67
  542.7 5.1 multiply_reduce_fusion
  548.0 0.9 copy.49
  (15 shorter events, 1.1 us)
Async XLA Ops:
  0.0 15.5 %copy-start = (bf16[2,512,256]{2,1,0:T(8,128)(2,1)S(1)}, bf16[2,512,256]{2,1,0:T(8,128)(2,1)}, u32[]{:S(2)}) copy-start(bf16[2,512,256]{2,1,0:T(8,128)(2,1)} %param.5) | copy-start | bytes 1572868
  5.3 130.9 %all-to-all-start = ((bf16[32,32,4096]{2,1,0:T(8,128)(2,1)}), bf16[32,32,4096]{2,1,0:T(8,128)(2,1)}, u32[]{:S(2)}, u32[]{:S(2)}) async-start(bf16[32,32,4096]{2,1,0:T(8,128)(2,1)} %stack.2), calls=%async_computation | async-start | bytes 16777216 | tf_op jit(solution)/shard_map/all_to_all | solution.py:46
  204.6 146.7 %all-to-all-start.1 = ((f32[128,1,256]{2,1,0:T(1,128)}), f32[128,1,256]{2,1,0:T(1,128)S(1)}, u32[]{:S(2)}, u32[]{:S(2)}) async-start(f32[128,1,256]{2,1,0:T(1,128)} %reshape.96), calls=%async_computation.1 | async-start | bytes 262144 | tf_op jit(solution)/shard_map/all_to_all | solution.py:57
  351.3 134.1 %all-to-all-start.2 = ((bf16[128,2,16384]{2,1,0:T(2,128)(2,1)}), bf16[128,2,16384]{2,1,0:T(2,128)(2,1)}, u32[]{:S(2)}, u32[]{:S(2)}) async-start(bf16[128,2,16384]{2,1,0:T(2,128)(2,1)} %reshape.94), calls=%async_computation.2 | async-start | bytes 16777216 | tf_op jit(solution)/shard_map/all_to_all | solution.py:54
